TPU v7x, 32 devices: a whole 2x2x4 slice. The times are simulated.
32 devices in a mesh: ha: 8 (over y, x, core), col: 4 (over z).
Axes of the slice: x: 2, y: 2, z: 4, core: 2. Of those that a mesh axis runs over, the one named last changes fastest.
Arguments:
- features: bfloat16 [3, 32, 128, 512], P(None, 'ha', 'col'), may hold values from -18 to 18
Outputs:
- lag_cov: float32 [128, 16000], P('col', 'ha')
All inputs are finite; a program needn't handle non-finite values.
Results may differ from a plain program's by a relative error of at most 0.0003.
Values may be sent and summed in bfloat16 or wider, within the bound.
A program may use at most 384 MiB of HBM per device.

v0:
```python
import functools

import jax
import jax.numpy as jnp
from jax import lax
from jax.experimental import pallas as pl
from jax.experimental.pallas import tpu as pltpu
from jax.sharding import PartitionSpec as P

MESH = pl.DeviceIdType.MESH
REACH = 2
STEPS = 2 * REACH + 1


def window_plan(lag_count, channels, ha_count):
    share = lag_count * channels // ha_count
    spans = [-(-(i + 1) * share // channels) - i * share // channels for i in range(ha_count)]
    return share, max(spans)


def kernel(
    ha_count, col_count, x_ref, out_ref, base, stack, others, part, near, mixed, far, summed, early,
    local_sem, halo_send, halo_recv, line_send, line_recv, near_send, near_recv, far_send, far_recv,
):
    frames, rows, block, width = x_ref.shape
    channels = block * col_count
    lag_count = STEPS**3
    share, span = window_plan(lag_count, channels, ha_count)
    i, j = lax.axis_index("ha"), lax.axis_index("col")
    half = ha_count // 2
    parity, place = lax.rem(i, 2), lax.div(i, 2)
    partner = i + 1 - 2 * parity

    def first_lag(index):
        return jnp.minimum(lax.div(index * share, channels), lag_count - span)

    barrier = pltpu.get_barrier_semaphore()
    for step in range(1, ha_count):
        pl.semaphore_signal(
            barrier, inc=1, device_id={"ha": lax.rem(i + step, ha_count)}, device_id_type=MESH
        )

    @pl.when(j > 0)
    def _():
        pl.semaphore_signal(barrier, inc=1, device_id={"col": j - 1}, device_id_type=MESH)

    @pl.when(j < col_count - 1)
    def _():
        pl.semaphore_signal(barrier, inc=1, device_id={"col": j + 1}, device_id_type=MESH)

    own_copies = []
    for h in range(rows):
        own_copies.append(
            pltpu.make_async_copy(
                x_ref.at[:, h], others.at[h, j], local_sem.at[0, h]
            )
        )
        own_copies.append(
            pltpu.make_async_copy(
                x_ref.at[:, h], base.at[:, :, pl.ds((h + REACH) * width, width)], local_sem.at[1, h]
            )
        )
    for copy in own_copies:
        copy.start()

    ends = (j > 0).astype(jnp.int32) + (j < col_count - 1).astype(jnp.int32)
    pl.semaphore_wait(barrier, ha_count - 1 + ends)

    def halo(way, r):
        source = rows - REACH + r if way == 0 else r
        slot = r if way == 0 else rows + REACH + r
        return pltpu.make_async_remote_copy(
            src_ref=x_ref.at[:, source],
            dst_ref=base.at[:, :, pl.ds(slot * width, width)],
            send_sem=halo_send.at[way, r],
            recv_sem=halo_recv.at[way, r],
            device_id={"ha": (i + 1) if way == 0 else (i - 1)},
            device_id_type=MESH,
        )

    def hop(way, step, h):
        sign = 1 if way == 0 else -1
        owner = j - sign * step
        return pltpu.make_async_remote_copy(
            src_ref=x_ref.at[:, h] if step == 0 else others.at[h, owner],
            dst_ref=others.at[h, owner],
            send_sem=line_send.at[way, step, h],
            recv_sem=line_recv.at[way, step, h],
            device_id={"col": j + sign},
            device_id_type=MESH,
        )

    def sends(way, step):
        if way == 0:
            return jnp.logical_and(j < col_count - 1, j - step >= 0)
        return jnp.logical_and(j > 0, j + step <= col_count - 1)

    def receives(way, step):
        return j - 1 - step >= 0 if way == 0 else j + 1 + step <= col_count - 1

    def arrival(way, step, h):
        sign = 1 if way == 0 else -1
        owner = j - sign * (step + 1)
        return pltpu.make_async_remote_copy(
            src_ref=others.at[h, owner],
            dst_ref=others.at[h, owner],
            send_sem=line_send.at[way, step, h],
            recv_sem=line_recv.at[way, step, h],
            device_id={"col": j - sign},
            device_id_type=MESH,
        )

    for way in range(2):

        @pl.when(sends(way, 0))
        def _():
            for h in range(rows):
                hop(way, 0, h).start()

    has_after, has_before = i < ha_count - 1, i > 0
    for way, has in ((0, has_after), (1, has_before)):

        @pl.when(has)
        def _():
            for r in range(REACH):
                halo(way, r).start()

    for copy in own_copies:
        copy.wait()

    @pl.when(jnp.logical_not(has_before))
    def _():
        base[:, :, : REACH * width] = jnp.zeros((frames, block, REACH * width), base.dtype)

    @pl.when(jnp.logical_not(has_after))
    def _():
        base[:, :, (rows + REACH) * width :] = jnp.zeros((frames, block, REACH * width), base.dtype)

    for way, has_in in ((0, has_before), (1, has_after)):

        @pl.when(has_in)
        def _():
            for r in range(REACH):
                halo(way, r).wait_recv()

    column = lax.broadcasted_iota(jnp.int32, (block, width), 1)

    def shift_row(index, carry):
        t, h = lax.div(index, rows + 2 * REACH), lax.rem(index, rows + 2 * REACH)
        lanes = pl.ds(pl.multiple_of(h * width, width), width)
        plain = base[t, :, lanes]
        wide = plain.astype(jnp.float32)
        for step_w in range(STEPS):
            shift = step_w - REACH
            if shift == 0:
                stack[step_w, t, :, lanes] = plain
            else:
                moved = pltpu.roll(wide, shift % width, axis=1)
                keep = column >= shift if shift > 0 else column < width + shift
                stack[step_w, t, :, lanes] = jnp.where(keep, moved, 0.0).astype(plain.dtype)
        return carry

    lax.fori_loop(0, frames * (rows + 2 * REACH), shift_row, 0)

    def advance(step, first, last):
        for h in range(first, last):
            for way in range(2):

                @pl.when(receives(way, step))
                def _():
                    arrival(way, step, h).wait_recv()

                if step + 1 < col_count - 1:

                    @pl.when(sends(way, step + 1))
                    def _():
                        hop(way, step + 1, h).start()

    both = jnp.minimum(j, col_count - 1 - j)
    more_after = j < col_count - 1 - j

    def owner_of(slot):
        paired = j + ((slot + 1) // 2) * (1 if slot % 2 == 0 else -1)
        single = jnp.where(more_after, j + (slot - both), j - (slot - both))
        return jnp.where(slot <= 2 * both, paired, single)

    group = block // col_count
    scale = 1.0 / (frames * rows * ha_count * width)
    lane_block = lax.broadcasted_iota(jnp.int32, (group, channels), 1) // block

    def compute(slot, first, last):
        depth = (last - first) * width
        owner = owner_of(slot)

        def products(step_h, carry):
            start = pl.multiple_of((STEPS - 1 - step_h + first) * width, width)
            own = stack[:, :, :, pl.ds(start, depth)].reshape(STEPS * frames * block, depth)
            field = jnp.concatenate(
                [others[h, owner].reshape(frames * block, width) for h in range(first, last)], axis=1
            )
            result = lax.dot_general(
                own, field, (((1,), (1,)), ((), ())), preferred_element_type=jnp.float32
            )
            if first > 0:
                result = result + early[step_h]
            if last < rows:
                early[step_h] = result
                return carry
            spare = jnp.zeros((result.shape[0], channels - result.shape[1]), jnp.float32)
            result = jnp.concatenate([result * scale, spare], axis=1)
            moved = [result] + [pltpu.roll(result, k * block, axis=1) for k in range(1, col_count)]
            for step_w in range(STEPS):
                for step_t in range(STEPS):
                    shift = step_t - REACH
                    packed = jnp.zeros((group, channels), jnp.float32)
                    for g in range(col_count):
                        total = None
                        for t in range(frames):
                            if 0 <= t + shift < frames:
                                row = (step_w * frames + t) * block + g * group
                                term = moved[(g - t - shift) % col_count][row : row + group]
                                total = term if total is None else total + term
                        if total is not None:
                            packed = jnp.where(lane_block == g, total, packed)
                    part[slot, step_t * STEPS * STEPS + step_h * STEPS + step_w] = packed
            return carry

        lax.fori_loop(0, STEPS, products, 0)

    near_copies, far_copies = {}, {}

    turns = [*range(1, half), 0]

    def pass_near(slot):
        for r in turns:
            target = lax.rem(place + r, half)
            near_copies[slot, r] = pltpu.make_async_remote_copy(
                src_ref=part.at[slot, pl.ds(first_lag(2 * target + 1 - parity), span)],
                dst_ref=near.at[slot, r],
                send_sem=near_send.at[slot, r],
                recv_sem=near_recv.at[slot, r],
                device_id={"ha": partner},
                device_id_type=MESH,
            )
            near_copies[slot, r].start()

    def pass_far(slot):
        for r in turns:
            target = lax.rem(place + r, half)
            near_copies[slot, r].wait_recv()
            mixed[slot, r] = part[slot, pl.ds(first_lag(2 * target + parity), span)] + near[slot, r]
            if r > 0:
                far_copies[slot, r] = pltpu.make_async_remote_copy(
                    src_ref=mixed.at[slot, r],
                    dst_ref=far.at[slot, r - 1],
                    send_sem=far_send.at[slot, r - 1],
                    recv_sem=far_recv.at[slot, r - 1],
                    device_id={"ha": 2 * target + parity},
                    device_id_type=MESH,
                )
                far_copies[slot, r].start()

    cuts = sorted({0, rows // 2, rows - 1, rows})
    if col_count > 1:
        advance(0, 0, rows)
    for slot in range(col_count):
        if slot < 2:
            compute(slot, 0, rows)
            if slot > 0:
                pass_far(slot - 1)
        elif slot < col_count - 1:
            advance(slot - 1, 0, rows)
            pass_far(slot - 1)
            compute(slot, 0, rows)
        else:
            for first, last in zip(cuts, cuts[1:]):
                advance(slot - 1, first, last)
                if first == 0:
                    pass_far(slot - 1)
                compute(slot, first, last)
        pass_near(slot)
    pass_far(col_count - 1)

    for slot in range(col_count):
        for r in range(1, half):
            far_copies[slot, r].wait_recv()
        total = mixed[slot, 0]
        for r in range(1, half):
            total = total + far[slot, r - 1]
        summed[owner_of(slot)] = total

    for k in range(span):
        tiles = [summed[q, k] for q in range(col_count)]
        for g in range(col_count):
            rows_out = jnp.zeros((group, channels), jnp.float32)
            for q in range(col_count):
                turn = (q - g) * block % channels
                tile = pltpu.roll(tiles[q], turn, axis=1) if turn else tiles[q]
                rows_out = jnp.where(lane_block == q, tile, rows_out)
            out_ref[g * group : (g + 1) * group, k * channels : (k + 1) * channels] = rows_out

    for copy in list(far_copies.values()) + list(near_copies.values()):
        copy.wait_send()
    for step in range(col_count - 1):
        for way in range(2):

            @pl.when(sends(way, step))
            def _():
                for h in range(rows):
                    hop(way, step, h).wait_send()

    for way, has in ((0, has_after), (1, has_before)):

        @pl.when(has)
        def _():
            for r in range(REACH):
                halo(way, r).wait_send()


def body(ha_count, col_count, features):
    frames, rows, block, width = features.shape
    channels = block * col_count
    lag_count = STEPS**3
    share, span = window_plan(lag_count, channels, ha_count)
    half = ha_count // 2
    group = block // col_count
    dma = pltpu.SemaphoreType.DMA
    lines = max(col_count - 1, 1)
    window = pl.pallas_call(
        functools.partial(kernel, ha_count, col_count),
        out_shape=jax.ShapeDtypeStruct((block, span * channels), jnp.float32),
        in_specs=[pl.BlockSpec(memory_space=pl.ANY)],
        out_specs=pl.BlockSpec(memory_space=pltpu.VMEM),
        scratch_shapes=[
            pltpu.VMEM((frames, block, (rows + 2 * REACH) * width), features.dtype),
            pltpu.VMEM((STEPS, frames, block, (rows + 2 * REACH) * width), features.dtype),
            pltpu.VMEM((rows, col_count, frames, block, width), features.dtype),
            pltpu.VMEM((col_count, lag_count, group, channels), jnp.float32),
            pltpu.VMEM((col_count, half, span, group, channels), jnp.float32),
            pltpu.VMEM((col_count, half, span, group, channels), jnp.float32),
            pltpu.VMEM((col_count, half, span, group, channels), jnp.float32),
            pltpu.VMEM((col_count, span, group, channels), jnp.float32),
            pltpu.VMEM((STEPS, STEPS * frames * block, frames * block), jnp.float32),
            dma((2, rows)),
            dma((2, REACH)),
            dma((2, REACH)),
            dma((2, lines, rows)),
            dma((2, lines, rows)),
            dma((col_count, half)),
            dma((col_count, half)),
            dma((col_count, half)),
            dma((col_count, half)),
        ],
        compiler_params=pltpu.CompilerParams(collective_id=0, has_side_effects=True),
        name="lag_cov",
    )(features)
    i = lax.axis_index("ha")
    first = jnp.minimum(i * share // channels, lag_count - span)
    return lax.dynamic_slice_in_dim(window, i * share - first * channels, share, 1)


def solution(mesh):
    in_specs = (P(None, "ha", "col", None),)
    out_specs = P("col", "ha")
    counts = (mesh.shape["ha"], mesh.shape["col"])
    return jax.shard_map(
        functools.partial(body, *counts), mesh=mesh, in_specs=in_specs, out_specs=out_specs, check_vma=False
    )
```

profile of v0, /device:TPU:0, one launch (start us, length us, event | category | flops | bytes accessed | tf_op | source)
XLA Modules:
  0.0 44.8 jit_solution(10189353918261410265)
XLA Ops:
  0.0 43.0 %lag_cov.1 = f32[32,2176]{1,0:T(8,128)} custom-call(bf16[3,4,32,512]{3,2,1,0:T(8,128)(2,1)} %x_ref.1), custom_call_target="tpu_custom_call" | custom-call | tf_op jit(solution)/shard_map/lag_cov/pallas_call | solution.py:329
  43.0 1.8 %constant_dynamic-slice_fusion = f32[32,2000]{1,0:T(8,128)} fusion(f32[32,2176]{1,0:T(8,128)} %lag_cov.1, s32[]{:T(128)S(6)} %select_n.9), kind=kLoop, calls=%fused_computation | loop fusion | bytes 512004 | tf_op jit(solution)/shard_map/dynamic_slice | solution.py:359
where the time goes:
time: 44.9 us; the launch traced here: 44.8 us
  Pallas kernels  43 us (96%)
  local copies, waits for them, and re-layouts  1.8 us (4%)
    pallas_call x1, Pallas kernels, body(): pl.pallas_call(functools.partial(kernel, ha_count, col_count), out_shape=...  43 us
    dynamic_slice x1, local copies, waits for them, and re-layouts, body(): lax.dynamic_slice_in_dim(window, i * share - first * channels, share, 1)  1.8 us

commit v1 on v0

v1 whole, which is shorter than its diff:
```python
import functools

import jax
import jax.numpy as jnp
from jax import lax
from jax.experimental import pallas as pl
from jax.experimental.pallas import tpu as pltpu
from jax.sharding import PartitionSpec as P

MESH = pl.DeviceIdType.MESH
REACH = 2
STEPS = 2 * REACH + 1


def window_plan(lag_count, channels, ha_count):
    share = lag_count * channels // ha_count
    spans = [-(-(i + 1) * share // channels) - i * share // channels for i in range(ha_count)]
    return share, max(spans)


def kernel(
    ha_count, col_count, x_ref, out_ref, stack, others, acc, part, near, mixed, far, summed, direct, turned,
    edges, edge_left, edge_own,
    local_sem, halo_send, halo_recv, line_send, line_recv, near_send, near_recv, far_send, far_recv,
    direct_send, direct_recv, turned_send, turned_recv, edge_send, edge_recv,
):
    frames, rows, block, width = x_ref.shape
    channels = block * col_count
    lag_count = STEPS**3
    share, span = window_plan(lag_count, channels, ha_count)
    i, j = lax.axis_index("ha"), lax.axis_index("col")
    half = ha_count // 2
    parity, place = lax.rem(i, 2), lax.div(i, 2)
    partner = i + 1 - 2 * parity
    mirror = ha_count - 1 - i
    middle = col_count // 2
    cut = width // 2
    frame_rows = frames * block

    def first_lag(index):
        return jnp.minimum(lax.div(index * share, channels), lag_count - span)

    barrier = pltpu.get_barrier_semaphore()
    for step in range(1, ha_count):
        pl.semaphore_signal(
            barrier, inc=1, device_id={"ha": lax.rem(i + step, ha_count)}, device_id_type=MESH
        )

    @pl.when(j > 0)
    def _():
        pl.semaphore_signal(barrier, inc=1, device_id={"col": j - 1}, device_id_type=MESH)

    @pl.when(j < col_count - 1)
    def _():
        pl.semaphore_signal(barrier, inc=1, device_id={"col": j + 1}, device_id_type=MESH)

    own_copies = [
        pltpu.make_async_copy(x_ref.at[:, h], stack.at[REACH + h, REACH], local_sem.at[h])
        for h in range(rows)
    ]
    for copy in own_copies:
        copy.start()

    ends = (j > 0).astype(jnp.int32) + (j < col_count - 1).astype(jnp.int32)
    pl.semaphore_wait(barrier, ha_count - 1 + ends)

    def halo(way, r):
        source = rows - REACH + r if way == 0 else r
        slot = r if way == 0 else rows + REACH + r
        return pltpu.make_async_remote_copy(
            src_ref=x_ref.at[:, source],
            dst_ref=stack.at[slot, REACH],
            send_sem=halo_send.at[way, r],
            recv_sem=halo_recv.at[way, r],
            device_id={"ha": (i + 1) if way == 0 else (i - 1)},
            device_id_type=MESH,
        )

    rest = max(col_count - 1, 1)

    def lanes_of(way):
        return pl.ds(cut, cut) if way == 0 else pl.ds(0, cut)

    def hop(way, step, h):
        sign = 1 if way == 0 else -1
        fresh = step in (0, rest)
        owner = j if fresh else j - sign * step
        lanes = lanes_of(1 - way if step == rest else way)
        return pltpu.make_async_remote_copy(
            src_ref=x_ref.at[:, h, :, lanes] if fresh else others.at[owner, h, :, :, lanes],
            dst_ref=others.at[owner, h, :, :, lanes],
            send_sem=line_send.at[way, step, h],
            recv_sem=line_recv.at[way, step, h],
            device_id={"col": j + sign},
            device_id_type=MESH,
        )

    def edge_hop(step):
        return pltpu.make_async_remote_copy(
            src_ref=edges.at[j - step],
            dst_ref=edges.at[j - step],
            send_sem=edge_send.at[step],
            recv_sem=edge_recv.at[step],
            device_id={"col": j + 1},
            device_id_type=MESH,
        )

    def edge_arrival(step):
        owner = j - 1 - step
        return pltpu.make_async_remote_copy(
            src_ref=edges.at[owner],
            dst_ref=edges.at[owner],
            send_sem=edge_send.at[step],
            recv_sem=edge_recv.at[step],
            device_id={"col": j - 1},
            device_id_type=MESH,
        )

    def travels(way, owner):
        if way == 0:
            useful = True if col_count - 2 < middle else owner != col_count - 2
            return jnp.logical_and(owner >= 0, useful)
        useful = True if 1 >= middle else owner != 1
        return jnp.logical_and(owner <= col_count - 1, useful)

    def sends(way, step):
        if way == 0:
            return jnp.logical_and(j < col_count - 1, travels(0, j - step))
        return jnp.logical_and(j > 0, travels(1, j + step))

    def receives(way, step):
        return travels(0, j - 1 - step) if way == 0 else travels(1, j + 1 + step)

    def sends_rest(way):
        return j + 1 < middle if way == 0 else j - 1 >= middle

    def receives_rest(way):
        if way == 0:
            return jnp.logical_and(j >= 1, j < middle)
        return jnp.logical_and(j >= middle, j < col_count - 1)

    def arrival(way, step, h):
        sign = 1 if way == 0 else -1
        owner = j - sign * (1 if step == rest else step + 1)
        lanes = lanes_of(1 - way if step == rest else way)
        return pltpu.make_async_remote_copy(
            src_ref=others.at[owner, h, :, :, lanes],
            dst_ref=others.at[owner, h, :, :, lanes],
            send_sem=line_send.at[way, step, h],
            recv_sem=line_recv.at[way, step, h],
            device_id={"col": j - sign},
            device_id_type=MESH,
        )

    for way in range(2):

        @pl.when(sends(way, 0))
        def _():
            for h in range(rows):
                hop(way, 0, h).start()

    has_after, has_before = i < ha_count - 1, i > 0
    for way, has in ((0, has_after), (1, has_before)):

        @pl.when(has)
        def _():
            for r in range(REACH):
                halo(way, r).start()

    for way in range(2):

        @pl.when(sends_rest(way))
        def _():
            for h in range(rows):
                hop(way, rest, h).start()

    inner = jnp.minimum(j, col_count - 1 - j) >= 1
    low = j < middle
    same_side = jnp.where(low, j + 1 < middle, j - 1 >= middle)
    inward = jnp.where(low, 1, -1)
    both = jnp.minimum(j, col_count - 1 - j)

    def owner_of(slot):
        if slot == 0:
            return j
        paired = j + ((slot + 1) // 2) * (inward if slot % 2 == 1 else -inward)
        single = j + inward * (slot - both)
        return jnp.where(slot <= 2 * both, paired, single)

    def when_active(slot, action):
        if slot == 1:
            pl.when(jnp.logical_not(same_side))(action)
        else:
            action()

    for slot in range(col_count):
        owner = owner_of(slot)
        blank = jnp.zeros(direct.shape[1:], direct.dtype)
        if slot == 0:
            turned[owner] = blank
        elif slot == 1:

            @pl.when(same_side)
            def _():
                turned[owner] = blank

        elif slot == 2:

            @pl.when(inner)
            def _():
                direct[owner] = blank

    column = lax.broadcasted_iota(jnp.int32, (block, width), 1)

    def shift_row(row, t):
        plain = stack[row, REACH, t]
        wide = plain.astype(jnp.float32)
        for step_w in range(STEPS):
            shift = REACH - step_w
            if shift != 0:
                moved = pltpu.roll(wide, shift % width, axis=1)
                keep = column >= shift if shift > 0 else column < width + shift
                stack[row, step_w, t] = jnp.where(keep, moved, 0.0).astype(plain.dtype)

    def shift_rows(first, count):
        def step(index, carry):
            shift_row(first + lax.div(index, frames), lax.rem(index, frames))
            return carry

        lax.fori_loop(0, count * frames, step, 0)

    for copy in own_copies:
        copy.wait()

    edge_tile = pl.ds(cut - channels, channels)
    edge_lane = lax.broadcasted_iota(jnp.int32, (frame_rows, channels), 1)

    def gather_edge(field, count):
        total = jnp.zeros((frame_rows, channels), jnp.float32)
        for h in range(count):
            tile = field(h).reshape(frame_rows, channels).astype(jnp.float32)
            moved = pltpu.roll(tile, (REACH * (h + 1)) % channels, axis=1)
            total = jnp.where(edge_lane // REACH == h, moved, total)
        return total

    @pl.when(sends(0, 0))
    def _():
        own_edge = gather_edge(lambda h: stack[REACH + h, REACH, :, :, edge_tile], rows)
        edges[j] = own_edge.astype(edges.dtype).reshape(frames, block, channels)
        edge_hop(0).start()

    shift_rows(REACH, rows)

    def advance(step, part_rows):
        for h in part_rows:
            for way in range(2):

                @pl.when(receives(way, step))
                def _():
                    arrival(way, step, h).wait_recv()

                if step + 1 < col_count - 1:

                    @pl.when(sends(way, step + 1))
                    def _():
                        hop(way, step + 1, h).start()

        if part_rows[-1] == rows - 1:

            @pl.when(receives(0, step))
            def _():
                edge_arrival(step).wait_recv()

            if step + 1 < col_count - 1:

                @pl.when(sends(0, step + 1))
                def _():
                    edge_hop(step + 1).start()

    halves = list(range(rows))
    if col_count > 1:
        advance(0, halves)

    for way, has_in, place_row in ((0, has_before, 0), (1, has_after, rows + REACH)):

        @pl.when(has_in)
        def _():
            for r in range(REACH):
                halo(way, r).wait_recv()
            shift_rows(place_row, REACH)

        @pl.when(jnp.logical_not(has_in))
        def _():
            for r in range(REACH):
                stack[place_row + r] = jnp.zeros(stack.shape[1:], stack.dtype)

    group = block // col_count
    scale = 1.0 / (frames * rows * ha_count * width)
    lane_block = lax.broadcasted_iota(jnp.int32, (group, channels), 1) // block

    def products(field, lanes, depth):
        for r in range(rows + 2 * REACH):
            picked = range(max(0, r - 2 * REACH), min(rows - 1, r) + 1)
            left = jnp.concatenate([field(h).reshape(frame_rows, depth) for h in picked], axis=0)
            own = stack[r, :, :, :, lanes].reshape(STEPS * frame_rows, depth)
            result = lax.dot_general(
                left, own, (((1,), (1,)), ((), ())), preferred_element_type=jnp.float32
            )
            for place_in, h in enumerate(picked):
                piece = result[place_in * frame_rows : (place_in + 1) * frame_rows]
                outs = pl.ds(0, STEPS * frame_rows)
                if h == 0:
                    acc[r - h, :, outs] = piece
                else:
                    acc[r - h, :, outs] = acc[r - h, :, outs] + piece

    edge_first = (STEPS - REACH) * frame_rows // channels * channels
    edge_pad = (STEPS - REACH) * frame_rows - edge_first
    edge_outs = pl.ds(edge_first, STEPS * frame_rows - edge_first)

    def gather_own_edges():
        if edge_pad:
            edge_own[:edge_pad] = jnp.zeros((edge_pad, channels), edge_own.dtype)
        for step_w in range(STEPS - REACH, STEPS):
            found = gather_edge(lambda r: stack[r, step_w, :, :, edge_tile], rows + 2 * REACH)
            kept = jnp.where(edge_lane % REACH >= 2 * REACH - step_w, found, 0.0)
            row = edge_pad + (step_w - STEPS + REACH) * frame_rows
            edge_own[row : row + frame_rows] = kept.astype(edge_own.dtype)

    def add_edges(owner):
        @pl.when(owner < j)
        def _():
            edge_left[...] = edges[owner].reshape(frame_rows, channels).astype(jnp.float32)

        @pl.when(owner > j)
        def _():
            edge_left[...] = -gather_edge(lambda h: others[owner, h, :, :, edge_tile], rows)

        plain = edge_left[...]
        turned_edges = [plain] + [pltpu.roll(plain, REACH * b, axis=1) for b in range(1, STEPS)]
        left = jnp.concatenate([edge.astype(edge_own.dtype) for edge in turned_edges], axis=0)
        result = lax.dot_general(
            left, edge_own[...], (((1,), (1,)), ((), ())), preferred_element_type=jnp.float32
        )
        for b in range(STEPS):
            acc[b, :, edge_outs] = acc[b, :, edge_outs] + result[b * frame_rows : (b + 1) * frame_rows]

    def pack(slot):
        def step(step_h, carry):
            moved = []
            for tile in range(acc.shape[2] // channels):
                plain = acc[step_h, :, tile * channels : (tile + 1) * channels] * scale
                moved.append([plain] + [pltpu.roll(plain, k * block, axis=1) for k in range(1, col_count)])
            for step_w in range(STEPS):
                for step_t in range(STEPS):
                    shift = step_t - REACH
                    packed = None
                    for g in range(col_count):
                        total = None
                        for t in range(frames):
                            if 0 <= t + shift < frames:
                                spot = step_w * frames + t + shift
                                row = t * block + g * group
                                source = moved[spot // col_count][(g - spot) % col_count]
                                term = source[row : row + group]
                                total = term if total is None else total + term
                        if total is None:
                            total = jnp.zeros((group, channels), jnp.float32)
                        packed = total if packed is None else jnp.where(lane_block == g, total, packed)
                    part[slot, step_t * STEPS * STEPS + step_h * STEPS + step_w] = packed
            return carry

        lax.fori_loop(0, STEPS, step, 0)

    def half_slot(owner):
        lanes = pl.ds(pl.multiple_of(jnp.where(owner < j, cut, 0), cut), cut)
        products(lambda h: others[owner, h, :, :, lanes], lanes, cut)
        add_edges(owner)

    turns = [*range(1, half), 0]

    def near_copy(slot, r):
        target = lax.rem(place + r, half)
        return pltpu.make_async_remote_copy(
            src_ref=part.at[slot, pl.ds(first_lag(2 * target + 1 - parity), span)],
            dst_ref=near.at[slot, r],
            send_sem=near_send.at[slot, r],
            recv_sem=near_recv.at[slot, r],
            device_id={"ha": partner},
            device_id_type=MESH,
        )

    def far_copy(slot, r):
        target = lax.rem(place + r, half)
        return pltpu.make_async_remote_copy(
            src_ref=mixed.at[slot, r],
            dst_ref=far.at[slot, r - 1],
            send_sem=far_send.at[slot, r - 1],
            recv_sem=far_recv.at[slot, r - 1],
            device_id={"ha": 2 * target + parity},
            device_id_type=MESH,
        )

    def direct_copy(slot):
        owner = owner_of(slot)
        return pltpu.make_async_remote_copy(
            src_ref=summed.at[slot],
            dst_ref=direct.at[j],
            send_sem=direct_send.at[slot],
            recv_sem=direct_recv.at[j],
            device_id={"col": owner},
            device_id_type=MESH,
        )

    def direct_arrival(owner):
        return pltpu.make_async_remote_copy(
            src_ref=direct.at[owner],
            dst_ref=direct.at[owner],
            send_sem=direct_send.at[0],
            recv_sem=direct_recv.at[owner],
            device_id={"col": owner},
            device_id_type=MESH,
        )

    def turned_copy(slot):
        owner = owner_of(slot)
        return pltpu.make_async_remote_copy(
            src_ref=summed.at[slot],
            dst_ref=turned.at[owner],
            send_sem=turned_send.at[slot],
            recv_sem=turned_recv.at[slot],
            device_id={"ha": mirror},
            device_id_type=MESH,
        )

    def pass_near(slot):
        def action():
            for r in turns:
                near_copy(slot, r).start()

        when_active(slot, action)

    def pass_far(slot):
        def action():
            for r in turns:
                target = lax.rem(place + r, half)
                near_copy(slot, r).wait_recv()
                mixed[slot, r] = part[slot, pl.ds(first_lag(2 * target + parity), span)] + near[slot, r]
                if r > 0:
                    far_copy(slot, r).start()

        when_active(slot, action)

    def finish(slot):
        def action():
            total = mixed[slot, 0]
            for r in range(1, half):
                far_copy(slot, r).wait_recv()
                total = total + far[slot, r - 1]
            if slot == 0:
                direct[j] = total
            else:
                summed[slot] = total
                direct_copy(slot).start()
                turned_copy(slot).start()

        when_active(slot, action)

    products(lambda h: stack[REACH + h, REACH], pl.ds(0, width), width)
    if col_count > 2:
        advance(1, halves[: rows // 2])
    pack(0)
    pass_near(0)
    gather_own_edges()
    for slot in range(1, col_count):
        owner = owner_of(slot)
        if slot == 1:

            @pl.when(jnp.logical_not(same_side))
            def _():
                half_slot(owner)
                pack(slot)

            if col_count > 2:
                advance(1, halves[rows // 2 :])
        elif slot == 2:
            for way in range(2):

                @pl.when(receives_rest(way))
                def _():
                    for h in range(rows):
                        arrival(way, rest, h).wait_recv()

            @pl.when(inner)
            def _():
                products(lambda h: others[owner, h], pl.ds(0, width), width)

            @pl.when(jnp.logical_not(inner))
            def _():
                half_slot(owner)

            pack(slot)
        else:
            advance(slot - 1, halves)
            half_slot(owner)
            pack(slot)
        pass_near(slot)
        pass_far(slot - 1)
        if slot > 1:
            finish(slot - 2)
    if col_count > 1:
        pass_far(col_count - 1)
        finish(col_count - 2)
    finish(col_count - 1)

    def assemble(ref, index):
        tiles = [ref[q, index] for q in range(col_count)]
        lines = []
        for g in range(col_count):
            line = None
            for q in range(col_count):
                turn = (q - g) * block % channels
                tile = pltpu.roll(tiles[q], turn, axis=1) if turn else tiles[q]
                line = tile if line is None else jnp.where(lane_block == q, tile, line)
            lines.append(line)
        return lines

    for slot in range(1, col_count):
        owner = owner_of(slot)
        if slot == 2:
            pl.when(jnp.logical_not(inner))(lambda: direct_arrival(owner).wait_recv())
        else:
            direct_arrival(owner).wait_recv()
        when_active(slot, lambda: turned_copy(slot).wait_recv())

    reach_index = lag_count - 1 - first_lag(i) - first_lag(mirror)
    for base in range(0, span, col_count):
        taken = range(base, min(base + col_count, span))
        lines = []
        for k in taken:
            lines.extend(assemble(turned, jnp.clip(reach_index - k, 0, span - 1)))
        lines.extend([jnp.zeros((group, channels), jnp.float32)] * (channels // group - len(lines)))
        flipped = jnp.concatenate(lines, axis=0).T
        for at, k in enumerate(taken):
            plain = assemble(direct, k)
            for g in range(col_count):
                line = None
                for q in range(col_count):
                    row = q * block + g * group
                    turn = (q - at) * block % channels
                    tile = flipped[row : row + group]
                    tile = pltpu.roll(tile, turn, axis=1) if turn else tile
                    line = tile if line is None else jnp.where(lane_block == q, tile, line)
                out_ref[g * group : (g + 1) * group, k * channels : (k + 1) * channels] = plain[g] + line

    def settle(slot):
        def action():
            for r in turns:
                near_copy(slot, r).wait_send()
                if r > 0:
                    far_copy(slot, r).wait_send()
            if slot > 0:
                direct_copy(slot).wait_send()
                turned_copy(slot).wait_send()

        when_active(slot, action)

    for slot in range(col_count):
        settle(slot)
    for way in range(2):
        for step in range(col_count - 1):

            @pl.when(sends(way, step))
            def _():
                for h in range(rows):
                    hop(way, step, h).wait_send()

        @pl.when(sends_rest(way))
        def _():
            for h in range(rows):
                hop(way, rest, h).wait_send()

    for step in range(col_count - 1):

        @pl.when(sends(0, step))
        def _():
            edge_hop(step).wait_send()

    for way, has in ((0, has_after), (1, has_before)):

        @pl.when(has)
        def _():
            for r in range(REACH):
                halo(way, r).wait_send()


def body(ha_count, col_count, features):
    frames, rows, block, width = features.shape
    channels = block * col_count
    lag_count = STEPS**3
    share, span = window_plan(lag_count, channels, ha_count)
    half = ha_count // 2
    group = block // col_count
    dma = pltpu.SemaphoreType.DMA
    lines = max(col_count - 1, 1)
    lanes = -(-STEPS * frames * block // channels) * channels
    tiles = pltpu.VMEM((col_count, span, group, channels), jnp.float32)
    edge_first = (STEPS - REACH) * frames * block // channels * channels
    window = pl.pallas_call(
        functools.partial(kernel, ha_count, col_count),
        out_shape=pltpu.VMEM((block, span * channels), jnp.float32),
        in_specs=[pl.BlockSpec(memory_space=pl.ANY)],
        out_specs=pl.BlockSpec(memory_space=pltpu.VMEM),
        scratch_shapes=[
            pltpu.VMEM((rows + 2 * REACH, STEPS, frames, block, width), features.dtype),
            pltpu.VMEM((col_count, rows, frames, block, width), features.dtype),
            pltpu.VMEM((STEPS, frames * block, lanes), jnp.float32),
            pltpu.VMEM((col_count, lag_count, group, channels), jnp.float32),
            pltpu.VMEM((col_count, half, span, group, channels), jnp.float32),
            pltpu.VMEM((col_count, half, span, group, channels), jnp.float32),
            pltpu.VMEM((col_count, half, span, group, channels), jnp.float32),
            tiles,
            tiles,
            tiles,
            pltpu.VMEM((col_count, frames, block, channels), features.dtype),
            pltpu.VMEM((frames * block, channels), jnp.float32),
            pltpu.VMEM((STEPS * frames * block - edge_first, channels), features.dtype),
            dma((rows,)),
            dma((2, REACH)),
            dma((2, REACH)),
            dma((2, lines + 1, rows)),
            dma((2, lines + 1, rows)),
            dma((col_count, half)),
            dma((col_count, half)),
            dma((col_count, half)),
            dma((col_count, half)),
            dma((col_count,)),
            dma((col_count,)),
            dma((col_count,)),
            dma((col_count,)),
            dma((lines,)),
            dma((lines,)),
        ],
        compiler_params=pltpu.CompilerParams(collective_id=0, has_side_effects=True),
        name="lag_cov",
    )(features)
    i = lax.axis_index("ha")
    first = jnp.minimum(i * share // channels, lag_count - span)
    return lax.dynamic_slice_in_dim(window, i * share - first * channels, share, 1)


def solution(mesh):
    in_specs = (P(None, "ha", "col", None),)
    out_specs = P("col", "ha")
    counts = (mesh.shape["ha"], mesh.shape["col"])
    return jax.shard_map(
        functools.partial(body, *counts), mesh=mesh, in_specs=in_specs, out_specs=out_specs, check_vma=False
    )
```

time: 44.9 us -> 44.6 us (level)
  the two profiles are of different devices: /device:TPU:0 before, /device:TPU:13 now
where the time goes in v1:
time: 44.6 us; the launch traced here: 44.5 us
  Pallas kernels  43.6 us (98%)
  local copies, waits for them, and re-layouts  0.85 us (2%)
    pallas_call x1, Pallas kernels, body(): pl.pallas_call(functools.partial(kernel, ha_count, col_count), out_shape=...  43.6 us

profile of v1, /device:TPU:13, one launch (start us, length us, event | category | flops | bytes accessed | tf_op | source)
XLA Modules:
  0.0 44.5 jit_solution(14173984268806074037)
XLA Ops:
  0.0 43.6 %lag_cov.1 = f32[32,2176]{1,0:T(8,128)S(1)} custom-call(bf16[3,4,32,512]{3,2,1,0:T(8,128)(2,1)} %x_ref.1), custom_call_target="tpu_custom_call" | custom-call | tf_op jit(solution)/shard_map/lag_cov/pallas_call | solution.py:609
  43.6 0.8 %constant_dynamic-slice_fusion = f32[32,2000]{1,0:T(8,128)} fusion(f32[32,2176]{1,0:T(8,128)S(1)} %lag_cov.1, s32[]{:T(128)S(6)} %select_n.9), kind=kLoop, calls=%fused_computation | loop fusion | bytes 512004 | tf_op jit(solution)/shard_map/dynamic_slice | solution.py:649

commit v2 on v1

--- a/solution.py
+++ b/solution.py
@@ -167,13 +167,6 @@
             for r in range(REACH):
                 halo(way, r).start()
 
-    for way in range(2):
-
-        @pl.when(sends_rest(way))
-        def _():
-            for h in range(rows):
-                hop(way, rest, h).start()
-
     inner = jnp.minimum(j, col_count - 1 - j) >= 1
     low = j < middle
     same_side = jnp.where(low, j + 1 < middle, j - 1 >= middle)
@@ -181,11 +174,13 @@
     both = jnp.minimum(j, col_count - 1 - j)
 
     def owner_of(slot):
-        if slot == 0:
-            return j
-        paired = j + ((slot + 1) // 2) * (inward if slot % 2 == 1 else -inward)
-        single = j + inward * (slot - both)
-        return jnp.where(slot <= 2 * both, paired, single)
+        inwards = col_count - 1 - both
+        return jnp.where(slot <= inwards, j + inward * slot, j - inward * (slot - inwards))
+
+    def whole(slot):
+        if 1 <= col_count - slot < middle:
+            return both == col_count - slot
+        return None
 
     def when_active(slot, action):
         if slot == 1:
@@ -193,61 +188,66 @@
         else:
             action()
 
-    for slot in range(col_count):
-        owner = owner_of(slot)
-        blank = jnp.zeros(direct.shape[1:], direct.dtype)
-        if slot == 0:
-            turned[owner] = blank
-        elif slot == 1:
-
-            @pl.when(same_side)
-            def _():
-                turned[owner] = blank
-
-        elif slot == 2:
-
-            @pl.when(inner)
-            def _():
-                direct[owner] = blank
-
-    column = lax.broadcasted_iota(jnp.int32, (block, width), 1)
-
-    def shift_row(row, t):
-        plain = stack[row, REACH, t]
-        wide = plain.astype(jnp.float32)
-        for step_w in range(STEPS):
-            shift = REACH - step_w
-            if shift != 0:
-                moved = pltpu.roll(wide, shift % width, axis=1)
-                keep = column >= shift if shift > 0 else column < width + shift
-                stack[row, step_w, t] = jnp.where(keep, moved, 0.0).astype(plain.dtype)
+    blank = jnp.zeros(direct.shape[1:], direct.dtype)
+    turned[j] = blank
+    if col_count > 1:
+
+        @pl.when(same_side)
+        def _():
+            turned[j + inward] = blank
+
+    @pl.when(inner)
+    def _():
+        direct[j - inward] = blank
+
+    frame_lane = lax.broadcasted_iota(jnp.int32, (frame_rows, channels), 1)
 
     def shift_rows(first, count):
         def step(index, carry):
-            shift_row(first + lax.div(index, frames), lax.rem(index, frames))
+            row = first + index
+            plain = stack[row, REACH].reshape(frame_rows, width)
+            for step_w in range(STEPS):
+                shift = REACH - step_w
+                if shift != 0:
+                    moved = pltpu.roll(plain, shift % width, axis=1)
+                    if shift > 0:
+                        head = moved[:, :channels]
+                        head = jnp.where(frame_lane >= shift, head, jnp.zeros_like(head))
+                        moved = jnp.concatenate([head, moved[:, channels:]], axis=1)
+                    else:
+                        tail = moved[:, width - channels :]
+                        tail = jnp.where(frame_lane < channels + shift, tail, jnp.zeros_like(tail))
+                        moved = jnp.concatenate([moved[:, : width - channels], tail], axis=1)
+                    stack[row, step_w] = moved.reshape(frames, block, width)
             return carry
 
-        lax.fori_loop(0, count * frames, step, 0)
+        lax.fori_loop(0, count, step, 0)
 
     for copy in own_copies:
         copy.wait()
 
     edge_tile = pl.ds(cut - channels, channels)
-    edge_lane = lax.broadcasted_iota(jnp.int32, (frame_rows, channels), 1)
 
     def gather_edge(field, count):
-        total = jnp.zeros((frame_rows, channels), jnp.float32)
+        total = jnp.zeros((frame_rows, channels), stack.dtype)
         for h in range(count):
-            tile = field(h).reshape(frame_rows, channels).astype(jnp.float32)
+            tile = field(h).reshape(frame_rows, channels)
             moved = pltpu.roll(tile, (REACH * (h + 1)) % channels, axis=1)
-            total = jnp.where(edge_lane // REACH == h, moved, total)
+            total = jnp.where(frame_lane // REACH == h, moved, total)
         return total
 
     @pl.when(sends(0, 0))
     def _():
         own_edge = gather_edge(lambda h: stack[REACH + h, REACH, :, :, edge_tile], rows)
-        edges[j] = own_edge.astype(edges.dtype).reshape(frames, block, channels)
+        edges[j] = own_edge.reshape(frames, block, channels)
         edge_hop(0).start()
+
+    for way in range(2):
+
+        @pl.when(sends_rest(way))
+        def _():
+            for h in range(rows):
+                hop(way, rest, h).start()
 
     shift_rows(REACH, rows)
 
@@ -265,7 +265,7 @@
                     def _():
                         hop(way, step + 1, h).start()
 
-        if part_rows[-1] == rows - 1:
+        if rows - 1 in part_rows:
 
             @pl.when(receives(0, step))
             def _():
@@ -278,28 +278,9 @@
                     edge_hop(step + 1).start()
 
     halves = list(range(rows))
-    if col_count > 1:
-        advance(0, halves)
-
-    for way, has_in, place_row in ((0, has_before, 0), (1, has_after, rows + REACH)):
-
-        @pl.when(has_in)
-        def _():
-            for r in range(REACH):
-                halo(way, r).wait_recv()
-            shift_rows(place_row, REACH)
-
-        @pl.when(jnp.logical_not(has_in))
-        def _():
-            for r in range(REACH):
-                stack[place_row + r] = jnp.zeros(stack.shape[1:], stack.dtype)
-
-    group = block // col_count
-    scale = 1.0 / (frames * rows * ha_count * width)
-    lane_block = lax.broadcasted_iota(jnp.int32, (group, channels), 1) // block
-
-    def products(field, lanes, depth):
-        for r in range(rows + 2 * REACH):
+    def products(field, lanes, depth, places=None, seen=None):
+        seen = set() if seen is None else seen
+        for r in range(rows + 2 * REACH) if places is None else places:
             picked = range(max(0, r - 2 * REACH), min(rows - 1, r) + 1)
             left = jnp.concatenate([field(h).reshape(frame_rows, depth) for h in picked], axis=0)
             own = stack[r, :, :, :, lanes].reshape(STEPS * frame_rows, depth)
@@ -309,10 +290,42 @@
             for place_in, h in enumerate(picked):
                 piece = result[place_in * frame_rows : (place_in + 1) * frame_rows]
                 outs = pl.ds(0, STEPS * frame_rows)
-                if h == 0:
+                if r - h in seen:
+                    acc[r - h, :, outs] = acc[r - h, :, outs] + piece
+                else:
                     acc[r - h, :, outs] = piece
-                else:
-                    acc[r - h, :, outs] = acc[r - h, :, outs] + piece
+                    seen.add(r - h)
+
+    diagonal_seen = set()
+
+    def diagonal(places):
+        products(lambda h: stack[REACH + h, REACH], pl.ds(0, width), width, places, diagonal_seen)
+
+    inside = list(range(REACH, REACH + rows))
+    outside = [*range(REACH), *range(REACH + rows, rows + 2 * REACH)]
+    spread = [halves[n * rows // 4 : (n + 1) * rows // 4] for n in range(4)]
+    for quarter in range(3):
+        if col_count > 1:
+            advance(0, spread[quarter])
+        if quarter < 2:
+            diagonal(inside[quarter * rows // 2 : (quarter + 1) * rows // 2])
+
+    for way, has_in, place_row in ((0, has_before, 0), (1, has_after, rows + REACH)):
+
+        @pl.when(has_in)
+        def _():
+            for r in range(REACH):
+                halo(way, r).wait_recv()
+            shift_rows(place_row, REACH)
+
+        @pl.when(jnp.logical_not(has_in))
+        def _():
+            for r in range(REACH):
+                stack[place_row + r] = jnp.zeros(stack.shape[1:], stack.dtype)
+
+    group = block // col_count
+    scale = 1.0 / (frames * rows * ha_count * width)
+    lane_block = lax.broadcasted_iota(jnp.int32, (group, channels), 1) // block
 
     edge_first = (STEPS - REACH) * frame_rows // channels * channels
     edge_pad = (STEPS - REACH) * frame_rows - edge_first
@@ -323,14 +336,14 @@
             edge_own[:edge_pad] = jnp.zeros((edge_pad, channels), edge_own.dtype)
         for step_w in range(STEPS - REACH, STEPS):
             found = gather_edge(lambda r: stack[r, step_w, :, :, edge_tile], rows + 2 * REACH)
-            kept = jnp.where(edge_lane % REACH >= 2 * REACH - step_w, found, 0.0)
+            kept = jnp.where(frame_lane % REACH >= 2 * REACH - step_w, found, jnp.zeros_like(found))
             row = edge_pad + (step_w - STEPS + REACH) * frame_rows
-            edge_own[row : row + frame_rows] = kept.astype(edge_own.dtype)
+            edge_own[row : row + frame_rows] = kept
 
     def add_edges(owner):
         @pl.when(owner < j)
         def _():
-            edge_left[...] = edges[owner].reshape(frame_rows, channels).astype(jnp.float32)
+            edge_left[...] = edges[owner].reshape(frame_rows, channels)
 
         @pl.when(owner > j)
         def _():
@@ -338,7 +351,7 @@
 
         plain = edge_left[...]
         turned_edges = [plain] + [pltpu.roll(plain, REACH * b, axis=1) for b in range(1, STEPS)]
-        left = jnp.concatenate([edge.astype(edge_own.dtype) for edge in turned_edges], axis=0)
+        left = jnp.concatenate(turned_edges, axis=0)
         result = lax.dot_general(
             left, edge_own[...], (((1,), (1,)), ((), ())), preferred_element_type=jnp.float32
         )
@@ -347,26 +360,29 @@
 
     def pack(slot):
         def step(step_h, carry):
-            moved = []
-            for tile in range(acc.shape[2] // channels):
-                plain = acc[step_h, :, tile * channels : (tile + 1) * channels] * scale
-                moved.append([plain] + [pltpu.roll(plain, k * block, axis=1) for k in range(1, col_count)])
+            moved = {}
+            for t in range(frames):
+                for g in range(col_count):
+                    row = t * block + g * group
+                    turn = (g - t) % col_count * block
+                    for tile in range(acc.shape[2] // channels):
+                        piece = acc[step_h, row : row + group, tile * channels : (tile + 1) * channels]
+                        moved[t, g, tile] = pltpu.roll(piece, turn, axis=1) if turn else piece
             for step_w in range(STEPS):
                 for step_t in range(STEPS):
                     shift = step_t - REACH
+                    base = step_w * frames + shift
                     packed = None
                     for g in range(col_count):
                         total = None
-                        for t in range(frames):
-                            if 0 <= t + shift < frames:
-                                spot = step_w * frames + t + shift
-                                row = t * block + g * group
-                                source = moved[spot // col_count][(g - spot) % col_count]
-                                term = source[row : row + group]
-                                total = term if total is None else total + term
+                        for t in range(max(0, -shift), min(frames, frames - shift)):
+                            term = moved[t, g, (base + t) // col_count]
+                            total = term if total is None else total + term
                         if total is None:
                             total = jnp.zeros((group, channels), jnp.float32)
-                        packed = total if packed is None else jnp.where(lane_block == g, total, packed)
+                        packed = total if packed is None else jnp.where(lane_block == (base + g) % col_count, total, packed)
+                    turn = -base % col_count * block
+                    packed = pltpu.roll(packed, turn, axis=1) if turn else packed
                     part[slot, step_t * STEPS * STEPS + step_h * STEPS + step_w] = packed
             return carry
 
@@ -466,11 +482,18 @@
 
         when_active(slot, action)
 
-    products(lambda h: stack[REACH + h, REACH], pl.ds(0, width), width)
-    if col_count > 2:
-        advance(1, halves[: rows // 2])
+    if col_count > 1:
+        advance(0, spread[3])
+
+    def relay(quarter):
+        if col_count > 2:
+            advance(1, spread[quarter])
+
+    diagonal(outside)
     pack(0)
     pass_near(0)
+    relay(0)
+    relay(1)
     gather_own_edges()
     for slot in range(1, col_count):
         owner = owner_of(slot)
@@ -481,9 +504,20 @@
                 half_slot(owner)
                 pack(slot)
 
-            if col_count > 2:
-                advance(1, halves[rows // 2 :])
-        elif slot == 2:
+            pass_near(slot)
+            relay(2)
+            pass_far(0)
+            relay(3)
+            pass_far(slot)
+            continue
+        if slot > 2:
+
+            @pl.when(jnp.logical_not(inner))
+            def _():
+                pass_far(slot - 1)
+
+            advance(slot - 1, halves)
+        if slot == middle + 1:
             for way in range(2):
 
                 @pl.when(receives_rest(way))
@@ -491,26 +525,46 @@
                     for h in range(rows):
                         arrival(way, rest, h).wait_recv()
 
+        if whole(slot) is None:
+            half_slot(owner)
+        else:
+
+            @pl.when(whole(slot))
+            def _():
+                products(lambda h: others[owner, h], pl.ds(0, width), width)
+
+            @pl.when(jnp.logical_not(whole(slot)))
+            def _():
+                half_slot(owner)
+
+        pack(slot)
+        pass_near(slot)
+        if slot > 2:
+
             @pl.when(inner)
             def _():
-                products(lambda h: others[owner, h], pl.ds(0, width), width)
-
-            @pl.when(jnp.logical_not(inner))
-            def _():
-                half_slot(owner)
-
-            pack(slot)
-        else:
-            advance(slot - 1, halves)
-            half_slot(owner)
-            pack(slot)
-        pass_near(slot)
-        pass_far(slot - 1)
-        if slot > 1:
+                pass_far(slot - 1)
+
             finish(slot - 2)
-    if col_count > 1:
+            if slot == col_count - 1:
+
+                @pl.when(jnp.logical_not(inner))
+                def _():
+                    finish(slot - 1)
+
+        if slot == 2:
+            finish(0)
+    if col_count > 2:
         pass_far(col_count - 1)
-        finish(col_count - 2)
+
+        @pl.when(inner)
+        def _():
+            finish(col_count - 2)
+
+    elif col_count > 1:
+        finish(0)
+    else:
+        pass_far(0)
     finish(col_count - 1)
 
     def assemble(ref, index):
@@ -527,10 +581,10 @@
 
     for slot in range(1, col_count):
         owner = owner_of(slot)
-        if slot == 2:
-            pl.when(jnp.logical_not(inner))(lambda: direct_arrival(owner).wait_recv())
+        if whole(slot) is None:
+            direct_arrival(owner).wait_recv()
         else:
-            direct_arrival(owner).wait_recv()
+            pl.when(jnp.logical_not(whole(slot)))(lambda: direct_arrival(owner).wait_recv())
         when_active(slot, lambda: turned_copy(slot).wait_recv())
 
     reach_index = lag_count - 1 - first_lag(i) - first_lag(mirror)
@@ -551,7 +605,7 @@
                     tile = flipped[row : row + group]
                     tile = pltpu.roll(tile, turn, axis=1) if turn else tile
                     line = tile if line is None else jnp.where(lane_block == q, tile, line)
-                out_ref[g * group : (g + 1) * group, k * channels : (k + 1) * channels] = plain[g] + line
+                out_ref[g * group : (g + 1) * group, k * channels : (k + 1) * channels] = (plain[g] + line) * scale
 
     def settle(slot):
         def action():
@@ -623,7 +677,7 @@
             tiles,
             tiles,
             pltpu.VMEM((col_count, frames, block, channels), features.dtype),
-            pltpu.VMEM((frames * block, channels), jnp.float32),
+            pltpu.VMEM((frames * block, channels), features.dtype),
             pltpu.VMEM((STEPS * frames * block - edge_first, channels), features.dtype),
             dma((rows,)),
             dma((2, REACH)),

time: 44.6 us -> 40.6 us (0.910)
  the two profiles are of different devices: /device:TPU:13 before, /device:TPU:0 now
where the time goes in v2:
time: 40.6 us; the launch traced here: 40.5 us
  Pallas kernels  39.6 us (98%)
  local copies, waits for them, and re-layouts  0.85 us (2%)
    pallas_call x1, Pallas kernels, body(): pl.pallas_call(functools.partial(kernel, ha_count, col_count), out_shape=...  39.6 us
    dynamic_slice x1, local copies, waits for them, and re-layouts, body(): lax.dynamic_slice_in_dim(window, i * share - first * channels, share, 1)  0.85 us

profile of v2, /device:TPU:0, one launch (start us, length us, event | category | flops | bytes accessed | tf_op | source)
XLA Modules:
  0.0 40.5 jit_solution(8465733122662900726)
XLA Ops:
  0.0 39.6 %lag_cov.1 = f32[32,2176]{1,0:T(8,128)S(1)} custom-call(bf16[3,4,32,512]{3,2,1,0:T(8,128)(2,1)} %x_ref.1), custom_call_target="tpu_custom_call" | custom-call | tf_op jit(solution)/shard_map/lag_cov/pallas_call | solution.py:663
  39.6 0.8 %constant_dynamic-slice_fusion = f32[32,2000]{1,0:T(8,128)} fusion(f32[32,2176]{1,0:T(8,128)S(1)} %lag_cov.1, s32[]{:T(128)S(6)} %select_n.9), kind=kLoop, calls=%fused_computation | loop fusion | bytes 512004 | tf_op jit(solution)/shard_map/dynamic_slice | solution.py:703

commit v3 on v2

--- a/solution.py
+++ b/solution.py
@@ -33,6 +33,7 @@
     parity, place = lax.rem(i, 2), lax.div(i, 2)
     partner = i + 1 - 2 * parity
     mirror = ha_count - 1 - i
+    pieces = [pl.ds(0, -(-span // 2)), pl.ds(-(-span // 2), span // 2)][: min(span, 2)]
     middle = col_count // 2
     cut = width // 2
     frame_rows = frames * block
@@ -386,7 +387,7 @@
                     part[slot, step_t * STEPS * STEPS + step_h * STEPS + step_w] = packed
             return carry
 
-        lax.fori_loop(0, STEPS, step, 0)
+        lax.fori_loop(0, STEPS, step, 0, unroll=True)
 
     def half_slot(owner):
         lanes = pl.ds(pl.multiple_of(jnp.where(owner < j, cut, 0), cut), cut)
@@ -406,45 +407,45 @@
             device_id_type=MESH,
         )
 
-    def far_copy(slot, r):
+    def far_copy(slot, r, c):
         target = lax.rem(place + r, half)
         return pltpu.make_async_remote_copy(
-            src_ref=mixed.at[slot, r],
-            dst_ref=far.at[slot, r - 1],
-            send_sem=far_send.at[slot, r - 1],
-            recv_sem=far_recv.at[slot, r - 1],
+            src_ref=mixed.at[slot, r, pieces[c]],
+            dst_ref=far.at[slot, r - 1, pieces[c]],
+            send_sem=far_send.at[slot, r - 1, c],
+            recv_sem=far_recv.at[slot, r - 1, c],
             device_id={"ha": 2 * target + parity},
             device_id_type=MESH,
         )
 
-    def direct_copy(slot):
+    def direct_copy(slot, c):
         owner = owner_of(slot)
         return pltpu.make_async_remote_copy(
-            src_ref=summed.at[slot],
-            dst_ref=direct.at[j],
-            send_sem=direct_send.at[slot],
-            recv_sem=direct_recv.at[j],
+            src_ref=summed.at[slot, pieces[c]],
+            dst_ref=direct.at[j, pieces[c]],
+            send_sem=direct_send.at[slot, c],
+            recv_sem=direct_recv.at[j, c],
             device_id={"col": owner},
             device_id_type=MESH,
         )
 
-    def direct_arrival(owner):
-        return pltpu.make_async_remote_copy(
-            src_ref=direct.at[owner],
-            dst_ref=direct.at[owner],
-            send_sem=direct_send.at[0],
-            recv_sem=direct_recv.at[owner],
+    def direct_arrival(owner, c):
+        return pltpu.make_async_remote_copy(
+            src_ref=direct.at[owner, pieces[c]],
+            dst_ref=direct.at[owner, pieces[c]],
+            send_sem=direct_send.at[0, c],
+            recv_sem=direct_recv.at[owner, c],
             device_id={"col": owner},
             device_id_type=MESH,
         )
 
-    def turned_copy(slot):
+    def turned_copy(slot, c):
         owner = owner_of(slot)
         return pltpu.make_async_remote_copy(
-            src_ref=summed.at[slot],
-            dst_ref=turned.at[owner],
-            send_sem=turned_send.at[slot],
-            recv_sem=turned_recv.at[slot],
+            src_ref=summed.at[slot, pieces[c]],
+            dst_ref=turned.at[owner, pieces[c]],
+            send_sem=turned_send.at[slot, c],
+            recv_sem=turned_recv.at[slot, c],
             device_id={"ha": mirror},
             device_id_type=MESH,
         )
@@ -463,22 +464,26 @@
                 near_copy(slot, r).wait_recv()
                 mixed[slot, r] = part[slot, pl.ds(first_lag(2 * target + parity), span)] + near[slot, r]
                 if r > 0:
-                    far_copy(slot, r).start()
+                    far_copy(slot, r, 0).start()
+            for c in range(1, len(pieces)):
+                for r in range(1, half):
+                    far_copy(slot, r, c).start()
 
         when_active(slot, action)
 
     def finish(slot):
         def action():
-            total = mixed[slot, 0]
-            for r in range(1, half):
-                far_copy(slot, r).wait_recv()
-                total = total + far[slot, r - 1]
-            if slot == 0:
-                direct[j] = total
-            else:
-                summed[slot] = total
-                direct_copy(slot).start()
-                turned_copy(slot).start()
+            for c, piece in enumerate(pieces):
+                total = mixed[slot, 0, piece]
+                for r in range(1, half):
+                    far_copy(slot, r, c).wait_recv()
+                    total = total + far[slot, r - 1, piece]
+                if slot == 0:
+                    direct[j, piece] = total
+                else:
+                    summed[slot, piece] = total
+                    direct_copy(slot, c).start()
+                    turned_copy(slot, c).start()
 
         when_active(slot, action)
 
@@ -495,6 +500,7 @@
     relay(0)
     relay(1)
     gather_own_edges()
+    pass_far(0)
     for slot in range(1, col_count):
         owner = owner_of(slot)
         if slot == 1:
@@ -506,7 +512,6 @@
 
             pass_near(slot)
             relay(2)
-            pass_far(0)
             relay(3)
             pass_far(slot)
             continue
@@ -537,23 +542,27 @@
             def _():
                 half_slot(owner)
 
+        if slot > 2:
+
+            @pl.when(inner)
+            def _():
+                pass_far(slot - 1)
+                finish(slot - 2)
+
         pack(slot)
         pass_near(slot)
         if slot > 2:
 
-            @pl.when(inner)
+            @pl.when(jnp.logical_not(inner))
             def _():
-                pass_far(slot - 1)
-
-            finish(slot - 2)
+                finish(slot - 2)
+
             if slot == col_count - 1:
 
                 @pl.when(jnp.logical_not(inner))
                 def _():
                     finish(slot - 1)
 
-        if slot == 2:
-            finish(0)
     if col_count > 2:
         pass_far(col_count - 1)
 
@@ -565,6 +574,7 @@
         finish(0)
     else:
         pass_far(0)
+    finish(0)
     finish(col_count - 1)
 
     def assemble(ref, index):
@@ -581,11 +591,12 @@
 
     for slot in range(1, col_count):
         owner = owner_of(slot)
-        if whole(slot) is None:
-            direct_arrival(owner).wait_recv()
-        else:
-            pl.when(jnp.logical_not(whole(slot)))(lambda: direct_arrival(owner).wait_recv())
-        when_active(slot, lambda: turned_copy(slot).wait_recv())
+        for c in range(len(pieces)):
+            if whole(slot) is None:
+                direct_arrival(owner, c).wait_recv()
+            else:
+                pl.when(jnp.logical_not(whole(slot)))(lambda: direct_arrival(owner, c).wait_recv())
+            when_active(slot, lambda: turned_copy(slot, c).wait_recv())
 
     reach_index = lag_count - 1 - first_lag(i) - first_lag(mirror)
     for base in range(0, span, col_count):
@@ -611,11 +622,13 @@
         def action():
             for r in turns:
                 near_copy(slot, r).wait_send()
-                if r > 0:
-                    far_copy(slot, r).wait_send()
-            if slot > 0:
-                direct_copy(slot).wait_send()
-                turned_copy(slot).wait_send()
+                for c in range(len(pieces)):
+                    if r > 0:
+                        far_copy(slot, r, c).wait_send()
+            for c in range(len(pieces)):
+                if slot > 0:
+                    direct_copy(slot, c).wait_send()
+                    turned_copy(slot, c).wait_send()
 
         when_active(slot, action)
 
@@ -686,12 +699,12 @@
             dma((2, lines + 1, rows)),
             dma((col_count, half)),
             dma((col_count, half)),
-            dma((col_count, half)),
-            dma((col_count, half)),
-            dma((col_count,)),
-            dma((col_count,)),
-            dma((col_count,)),
-            dma((col_count,)),
+            dma((col_count, half, 2)),
+            dma((col_count, half, 2)),
+            dma((col_count, 2)),
+            dma((col_count, 2)),
+            dma((col_count, 2)),
+            dma((col_count, 2)),
             dma((lines,)),
             dma((lines,)),
         ],

time: 40.6 us -> 38.4 us (0.946)
  Pallas kernels: 39.6 us -> 37.4 us
    pallas_call x1, Pallas kernels: 39.6 us -> 37.4 us  [body(): pl.pallas_call(functools.partial(kernel, ha_count, col_count), out_shape=...]
where the time goes in v3:
time: 38.4 us; the launch traced here: 38.3 us
  Pallas kernels  37.4 us (97%)
  local copies, waits for them, and re-layouts  0.85 us (2%)
    pallas_call x1, Pallas kernels, body(): pl.pallas_call(functools.partial(kernel, ha_count, col_count), out_shape=...  37.4 us
    dynamic_slice x1, local copies, waits for them, and re-layouts, body(): lax.dynamic_slice_in_dim(window, i * share - first * channels, share, 1)  0.85 us

profile of v3, /device:TPU:0, one launch (start us, length us, event | category | flops | bytes accessed | tf_op | source)
XLA Modules:
  0.0 38.3 jit_solution(4448479029145509662)
XLA Ops:
  0.0 37.4 %lag_cov.1 = f32[32,2176]{1,0:T(8,128)S(1)} custom-call(bf16[3,4,32,512]{3,2,1,0:T(8,128)(2,1)} %x_ref.1), custom_call_target="tpu_custom_call" | custom-call | tf_op jit(solution)/shard_map/lag_cov/pallas_call | solution.py:676
  37.4 0.8 %constant_dynamic-slice_fusion = f32[32,2000]{1,0:T(8,128)} fusion(f32[32,2176]{1,0:T(8,128)S(1)} %lag_cov.1, s32[]{:T(128)S(6)} %select_n.9), kind=kLoop, calls=%fused_computation | loop fusion | bytes 512004 | tf_op jit(solution)/shard_map/dynamic_slice | solution.py:716

commit v4 on v3

--- a/solution.py
+++ b/solution.py
@@ -589,6 +589,44 @@
             lines.append(line)
         return lines
 
+    def settle(slot):
+        def action():
+            for r in turns:
+                near_copy(slot, r).wait_send()
+                for c in range(len(pieces)):
+                    if r > 0:
+                        far_copy(slot, r, c).wait_send()
+
+        when_active(slot, action)
+
+    for slot in range(col_count):
+        settle(slot)
+    for way in range(2):
+        for step in range(col_count - 1):
+
+            @pl.when(sends(way, step))
+            def _():
+                for h in range(rows):
+                    hop(way, step, h).wait_send()
+
+        @pl.when(sends_rest(way))
+        def _():
+            for h in range(rows):
+                hop(way, rest, h).wait_send()
+
+    for step in range(col_count - 1):
+
+        @pl.when(sends(0, step))
+        def _():
+            edge_hop(step).wait_send()
+
+    for way, has in ((0, has_after), (1, has_before)):
+
+        @pl.when(has)
+        def _():
+            for r in range(REACH):
+                halo(way, r).wait_send()
+
     for slot in range(1, col_count):
         owner = owner_of(slot)
         for c in range(len(pieces)):
@@ -618,47 +656,16 @@
                     line = tile if line is None else jnp.where(lane_block == q, tile, line)
                 out_ref[g * group : (g + 1) * group, k * channels : (k + 1) * channels] = (plain[g] + line) * scale
 
-    def settle(slot):
+    def settle_swap(slot):
         def action():
-            for r in turns:
-                near_copy(slot, r).wait_send()
-                for c in range(len(pieces)):
-                    if r > 0:
-                        far_copy(slot, r, c).wait_send()
             for c in range(len(pieces)):
-                if slot > 0:
-                    direct_copy(slot, c).wait_send()
-                    turned_copy(slot, c).wait_send()
+                direct_copy(slot, c).wait_send()
+                turned_copy(slot, c).wait_send()
 
         when_active(slot, action)
 
-    for slot in range(col_count):
-        settle(slot)
-    for way in range(2):
-        for step in range(col_count - 1):
-
-            @pl.when(sends(way, step))
-            def _():
-                for h in range(rows):
-                    hop(way, step, h).wait_send()
-
-        @pl.when(sends_rest(way))
-        def _():
-            for h in range(rows):
-                hop(way, rest, h).wait_send()
-
-    for step in range(col_count - 1):
-
-        @pl.when(sends(0, step))
-        def _():
-            edge_hop(step).wait_send()
-
-    for way, has in ((0, has_after), (1, has_before)):
-
-        @pl.when(has)
-        def _():
-            for r in range(REACH):
-                halo(way, r).wait_send()
+    for slot in range(1, col_count):
+        settle_swap(slot)
 
 
 def body(ha_count, col_count, features):

time: 38.4 us -> 38.3 us (level)
  no operation moved by 1% of the time
where the time goes in v4:
time: 38.3 us; the launch traced here: 38.2 us
  Pallas kernels  37.3 us (97%)
  local copies, waits for them, and re-layouts  0.85 us (2%)
    pallas_call x1, Pallas kernels, body(): pl.pallas_call(functools.partial(kernel, ha_count, col_count), out_shape=...  37.3 us
    dynamic_slice x1, local copies, waits for them, and re-layouts, body(): lax.dynamic_slice_in_dim(window, i * share - first * channels, share, 1)  0.85 us

profile of v4, /device:TPU:0, one launch (start us, length us, event | category | flops | bytes accessed | tf_op | source)
XLA Modules:
  0.0 38.2 jit_solution(16073998791333082813)
XLA Ops:
  0.0 37.3 %lag_cov.1 = f32[32,2176]{1,0:T(8,128)S(1)} custom-call(bf16[3,4,32,512]{3,2,1,0:T(8,128)(2,1)} %x_ref.1), custom_call_target="tpu_custom_call" | custom-call | tf_op jit(solution)/shard_map/lag_cov/pallas_call | solution.py:683
  37.3 0.8 %constant_dynamic-slice_fusion = f32[32,2000]{1,0:T(8,128)} fusion(f32[32,2176]{1,0:T(8,128)S(1)} %lag_cov.1, s32[]{:T(128)S(6)} %select_n.9), kind=kLoop, calls=%fused_computation | loop fusion | bytes 512004 | tf_op jit(solution)/shard_map/dynamic_slice | solution.py:723
